TPU v7x, 32 devices: a whole 2x2x4 slice. The times are simulated.
32 devices in a mesh: mem: 8 (over z, core), ma: 4 (over y, x).
Axes of the slice: x: 2, y: 2, z: 4, core: 2. Of those that a mesh axis runs over, the one named last changes fastest.
Arguments:
- ar_state: float32 [3, 32, 128, 2, 1280], P(None, 'mem', 'ma'), may hold values from -4 to 4
- forcing: float32 [3, 32, 128, 2, 1280], P(None, 'mem', 'ma'), may hold values from -6 to 6
- ar_decay: float32 [3], replicated, may hold values from 0.3 to 0.95
- amplitude: float32 [3, 1280], replicated, may hold values from 0.05 to 0.4
- wavenumber: int32 [128], replicated, may hold values from 0 to 1279, as said below
- tables: bfloat16 [128, 1280, 320], P('ma', None, 'mem'), may hold values from -0.15625 to 0.15625
- tendencies: bfloat16 [32, 320, 5120], P('mem', 'ma'), may hold values from -6 to 6
Outputs:
- perturbed: bfloat16 [32, 320, 5120], P('mem', 'ma')
- new_state: float32 [3, 32, 128, 2, 1280], P(None, 'mem', 'ma')
Inputs may be any that keep to these rules, and one draw needn't show every extreme that they name: `wavenumber`: 128 distinct values.
All inputs are finite; a program needn't handle non-finite values.
Results may differ from a plain program's by a relative error of at most 0.0042.
Values may be sent and summed in bfloat16 or wider, within the bound.
A program may use at most 64 MiB of HBM per device.

v0:
```python
import math

import jax
import jax.numpy as jnp
from jax import lax
from jax.sharding import PartitionSpec as P

clip_level = 0.9


def basis_table(wavenumber, lon_count):
    longitude = lax.broadcasted_iota(jnp.int32, (wavenumber.shape[0], lon_count), 1)
    phases = wavenumber[:, None] * longitude % lon_count
    angles = phases.astype(jnp.float32) * (2.0 * math.pi / lon_count)
    stacked = jnp.stack([jnp.cos(angles), -jnp.sin(angles)], axis=1)
    return stacked.reshape(2 * wavenumber.shape[0], lon_count).astype(jnp.bfloat16)


def per_device(ar_state, forcing, ar_decay, amplitude, wavenumber, tables, tendencies):
    local_waves = ar_state.shape[2]
    degree_count = ar_state.shape[4]
    owner_index = lax.axis_index("ma")
    own_waves = lax.dynamic_slice_in_dim(wavenumber, owner_index * local_waves, local_waves)
    degree_grid = lax.broadcasted_iota(jnp.int32, (local_waves, degree_count), 1)
    kept_mask = (degree_grid >= own_waves[:, None]).astype(jnp.float32)
    updated = (
        ar_decay[:, None, None, None, None] * ar_state + amplitude[:, None, None, None, :] * forcing
    )
    new_state = kept_mask[None, None, :, None, :] * updated
    coefficients = jnp.sum(new_state, axis=0).astype(jnp.bfloat16)
    everyone = lax.all_gather(coefficients, "mem", axis=0, tiled=True)
    product = jnp.einsum("bmcn,mnl->blmc", everyone, tables, preferred_element_type=jnp.float32)
    fourier = product.astype(jnp.bfloat16)
    banded = lax.all_to_all(
        lax.all_to_all(fourier, "mem", split_axis=0, concat_axis=1, tiled=True),
        "ma",
        split_axis=1,
        concat_axis=2,
        tiled=True,
    )
    member_count, lat_rows, window_size, reim_parts = banded.shape
    basis = basis_table(wavenumber, tendencies.shape[2])
    fourier_rows = banded.reshape(member_count * lat_rows, window_size * reim_parts)
    pattern = jnp.dot(fourier_rows, basis, preferred_element_type=jnp.float32) * (
        1.0 / math.sqrt(window_size)
    )
    pattern = jnp.clip(pattern, -clip_level, clip_level).reshape(tendencies.shape)
    perturbed = (tendencies.astype(jnp.float32) * (1.0 + pattern)).astype(jnp.bfloat16)
    return (perturbed, new_state)


def solution(mesh):
    return jax.shard_map(
        per_device,
        mesh=mesh,
        in_specs=(
            P(None, "mem", "ma", None, None),
            P(None, "mem", "ma", None, None),
            P(),
            P(),
            P(),
            P("ma", None, "mem"),
            P("mem", "ma", None),
        ),
        out_specs=(P("mem", "ma", None), P(None, "mem", "ma", None, None)),
        check_vma=False,
    )
```

profile of v0, /device:TPU:0, one launch (start us, length us, event | category | flops | bytes accessed | tf_op | source)
XLA Modules:
  0.0 144.6 jit_solution(2855487197622185122)
XLA Ops:
  7.2 0.0 copy-start
  7.2 0.0 all-gather.2.cloned.1.call-start
  7.2 0.9 dynamic_slice.3
  8.1 0.1 fusion.20
  8.2 9.1 %fusion.21 = (bf16[4,32,2,1280]{3,2,1,0:T(2,128)(2,1)S(1)}, f32[3,4,32,2,1280]{4,3,2,1,0:T(2,128)}) fusion(f32[3,4,32,2,1280]{4,3,2,1,0:T(2,128)} %param.8, f32[3,1280]{1,0:T(4,128)} %param.10, f32[3,4,32,2,1280]{4,3,2,1,0:T(2,128)} %param.7, f32[3]{0:T(128)} %param.9, f32[32,1280]{1,0:T(8,128)S(1)} %fusion.20), kind=kLoop, calls=%fused_computation.23 | loop fusion | flops 4587520 | bytes 12631052 | tf_op jit(solution)/shard_map/reduce_sum | solution.py:30
  17.3 0.9 copy.23
  18.2 0.0 all-gather.2.cloned.1.call-update
  18.2 0.0 copy-start.2
  18.2 58.8 %all-gather.2.cloned.1.call-done = bf16[32,32,2,1280]{3,1,2,0:T(8,128)(2,1)} async-done(((bf16[4,32,2,1280]{3,1,2,0:T(8,128)(2,1)}), bf16[32,32,2,1280]{3,1,2,0:T(8,128)(2,1)}) %all-gather.2.cloned.1.call-update) | async-done | bytes 5242896 | tf_op jit(solution)/shard_map/all_gather | solution.py:31
  77.1 0.0 copy-done
  77.1 5.6 %fusion.15 = bf16[32,40,32,2]{1,0,3,2:T(8,128)(2,1)S(1)} fusion(bf16[32,1280,40]{1,2,0:T(8,128)(2,1)S(1)} %copy-done, bf16[32,32,2,1280]{3,1,2,0:T(8,128)(2,1)} %all-gather.2.cloned.1.call-done), kind=kOutput, calls=%fused_computation.19 | convolution fusion | flops 209797120 | bytes 8683520 | tf_op jit(solution)/shard_map/bmcn,mnl->blmc/dot_general | solution.py:32
  82.6 1.3 copy.41
  84.0 2.5 %reshape.114 = bf16[8,2,5120]{2,1,0:T(2,128)(2,1)} reshape(bf16[32,32,2,40]{3,2,1,0:T(2,128)(2,1)} %bitcast.32) | data formatting | bytes 327680
  86.5 3.6 %all-to-all-start = ((bf16[8,2,5120]{2,1,0:T(2,128)(2,1)}), bf16[8,2,5120]{2,1,0:T(2,128)(2,1)S(1)}, u32[]{:S(2)}, u32[]{:S(2)}) async-start(bf16[8,2,5120]{2,1,0:T(2,128)(2,1)} %reshape.114), calls=%async_computation | async-start | bytes 327680 | tf_op jit(solution)/shard_map/all_to_all | solution.py:35
  90.0 0.0 copy-done.2
  90.0 13.1 %cosine_convert_fusion = (bf16[128,1,5120]{2,0,1:T(8,128)(2,1)}, bf16[128,1,5120]{2,0,1:T(8,128)(2,1)}) fusion(s32[128]{0:T(128)S(1)} %copy-done.2), kind=kLoop, calls=%fused_computation.13 | loop fusion | flops 7864320 | bytes 2621952 | tf_op jit(solution)/shard_map/convert
  103.1 0.0 all-to-all-done
  103.1 1.6 %reshape.115 = bf16[32,32,2,40]{3,2,1,0:T(2,128)(2,1)} reshape(bf16[8,2,5120]{2,1,0:T(2,128)(2,1)S(1)} %all-to-all-done) | data formatting | bytes 327680
  104.7 2.2 %copy.40 = bf16[8,4,40,32,2]{2,0,3,4,1:T(8,128)(2,1)} copy(bf16[8,4,40,32,2]{2,4,3,1,0:T(2,128)(2,1)} %bitcast.33) | data formatting | bytes 327680 | tf_op jit(solution)/shard_map/all_to_all | solution.py:35
  106.9 2.4 %copy.31 = bf16[4,8,40,32,2]{3,4,0,2,1:T(2,128)(2,1)} copy(bf16[4,8,40,32,2]{2,1,3,4,0:T(8,128)(2,1)} %bitcast.34) | data formatting | bytes 327680 | tf_op jit(solution)/shard_map/all_to_all | solution.py:35
  109.3 2.4 %reshape.116 = bf16[4,2,10240]{2,1,0:T(2,128)(2,1)} reshape(bf16[320,4,2,32]{3,2,1,0:T(2,128)(2,1)} %bitcast.30) | data formatting | bytes 327680
  111.7 3.6 %all-to-all-start.1 = ((bf16[4,2,10240]{2,1,0:T(2,128)(2,1)}), bf16[4,2,10240]{2,1,0:T(2,128)(2,1)S(1)}, u32[]{:S(2)}, u32[]{:S(2)}) async-start(bf16[4,2,10240]{2,1,0:T(2,128)(2,1)} %reshape.116), calls=%async_computation.1 | async-start | bytes 327680 | tf_op jit(solution)/shard_map/all_to_all | solution.py:34
  115.3 2.0 %pad_maximum_fusion = bf16[128,2,5120]{2,0,1:T(8,128)(2,1)S(1)} fusion(bf16[128,1,5120]{2,0,1:T(8,128)(2,1)} %get-tuple-element.5, bf16[128,1,5120]{2,0,1:T(8,128)(2,1)} %get-tuple-element.4), kind=kLoop, calls=%fused_computation.11 | loop fusion | flops 1310720 | bytes 5242880 | tf_op jit(solution)/shard_map/stack | solution.py:15
  117.3 4.2 %copy.29 = bf16[128,2,5120]{2,1,0:T(2,128)(2,1)} copy(bf16[128,2,5120]{2,0,1:T(8,128)(2,1)S(1)} %pad_maximum_fusion) | data formatting | bytes 5242880 | tf_op jit(solution)/shard_map/stack | solution.py:15
  121.4 6.5 %convert_element_type.52 = bf16[256,5120]{1,0:T(8,128)(2,1)} reshape(bf16[128,2,5120]{2,1,0:T(2,128)(2,1)} %copy.29) | data formatting | bytes 5242880 | tf_op jit(solution)/shard_map/convert_element_type | solution.py:16
  127.9 0.0 all-to-all-done.1
  127.9 1.2 reshape.117
  129.1 1.5 %copy.28 = bf16[4,4,80,32,2]{2,0,4,3,1:T(4,128)(2,1)S(1)} copy(bf16[4,4,80,32,2]{3,4,0,2,1:T(2,128)(2,1)} %bitcast.31) | data formatting | bytes 327680 | tf_op jit(solution)/shard_map/all_to_all | solution.py:34
  130.6 0.9 reshape.112
  131.5 0.0 copy-start.1
  131.5 3.5 %fusion.1 = f32[320,5120]{1,0:T(8,128)S(1)} fusion(bf16[320,256]{0,1:T(8,128)(2,1)} %reshape.112, bf16[256,5120]{1,0:T(8,128)(2,1)} %convert_element_type.52), kind=kOutput, calls=%fused_computation.2 | convolution fusion | flops 843776000 | bytes 9338880 | tf_op jit(solution)/shard_map/dot_general | solution.py:44
  135.0 0.0 copy-done.1
  135.0 2.7 %multiply_convert_fusion = bf16[4,80,5120]{2,1,0:T(8,128)(2,1)} fusion(f32[4,80,5120]{2,1,0:T(8,128)S(1)} %bitcast.29, bf16[4,80,5120]{2,1,0:T(8,128)(2,1)S(1)} %copy-done.1), kind=kLoop, calls=%fused_computation.3 | loop fusion | flops 4915200 | bytes 13107200 | tf_op jit(solution)/shard_map/convert_element_type | solution.py:48
Async XLA Ops:
  7.2 69.9 %copy-start = (bf16[32,1280,40]{1,2,0:T(8,128)(2,1)S(1)}, bf16[32,1280,40]{1,2,0:T(8,128)(2,1)}, u32[]{:S(2)}) copy-start(bf16[32,1280,40]{1,2,0:T(8,128)(2,1)} %param.12) | copy-start | bytes 9830404
  7.2 69.9 %all-gather.2.cloned.1.call-start = ((), (), s32[]{:S(2)}) async-start(), calls=%async_computation.2 | async-start | bytes 5898240 | tf_op jit(solution)/shard_map/all_gather | solution.py:31
  18.2 71.8 %copy-start.2 = (s32[128]{0:T(128)S(1)}, s32[128]{0:T(128)}, u32[]{:S(2)}) copy-start(s32[128]{0:T(128)} %param.11) | copy-start | bytes 1540
  86.5 16.7 %all-to-all-start = ((bf16[8,2,5120]{2,1,0:T(2,128)(2,1)}), bf16[8,2,5120]{2,1,0:T(2,128)(2,1)S(1)}, u32[]{:S(2)}, u32[]{:S(2)}) async-start(bf16[8,2,5120]{2,1,0:T(2,128)(2,1)} %reshape.114), calls=%async_computation | async-start | bytes 327680 | tf_op jit(solution)/shard_map/all_to_all | solution.py:35
  111.7 16.3 %all-to-all-start.1 = ((bf16[4,2,10240]{2,1,0:T(2,128)(2,1)}), bf16[4,2,10240]{2,1,0:T(2,128)(2,1)S(1)}, u32[]{:S(2)}, u32[]{:S(2)}) async-start(bf16[4,2,10240]{2,1,0:T(2,128)(2,1)} %reshape.116), calls=%async_computation.1 | async-start | bytes 327680 | tf_op jit(solution)/shard_map/all_to_all | solution.py:34
  131.5 3.5 %copy-start.1 = (bf16[4,80,5120]{2,1,0:T(8,128)(2,1)S(1)}, bf16[4,80,5120]{2,1,0:T(8,128)(2,1)}, u32[]{:S(2)}) copy-start(bf16[4,80,5120]{2,1,0:T(8,128)(2,1)} %param.13) | copy-start | bytes 9830404
Sparse Core Ops, SparseCore 0:
  18.3 58.6 all-gather.1
where the time goes:
time: 145 us
  waiting for transfers between devices  58.9 us (41%)
  local copies, waits for them, and re-layouts  28.3 us (20%)
  other arithmetic  26.9 us (19%)
  between operations  14.1 us (10%)
  matrix products  9.07 us (6%)
  starting transfers between devices  7.25 us (5%)
    all_gather x1, waiting for transfers between devices, per_device(): everyone = lax.all_gather(coefficients, 'mem', axis=0, tiled=True)  58.8 us
    another operation x1, other arithmetic  13.1 us
    reduce_sum x1, other arithmetic, per_device(): coefficients = jnp.sum(new_state, axis=0).astype(jnp.bfloat16)  9.09 us
    unnamed x10, local copies, waits for them, and re-layouts  7.6 us
    convert_element_type x1, local copies, waits for them, and re-layouts, basis_table(): stacked.reshape(2 * wavenumber.shape[0], lon_count).astype(jnp.bfloat16)  6.47 us
    dot_general x1, matrix products, per_device(): jnp.einsum('bmcn,mnl->blmc', everyone, tables, preferred_element_type=jnp...  5.56 us
    all_to_all x2, local copies, waits for them, and re-layouts, per_device(): lax.all_to_all(fourier, 'mem', split_axis=0, concat_axis=1, tiled=True)  4.56 us
    another operation x1, local copies, waits for them, and re-layouts, basis_table(): stacked = jnp.stack([jnp.cos(angles), -jnp.sin(angles)], axis=1)  4.19 us
  transfers between devices with their start and end apart: 3, of which 1 were waited for; matrix products, arithmetic and copies ran while one was open for 18% of the time, Pallas kernels for 0%

commit v1 on v0

v1 whole, which is shorter than its diff:
```python
import functools
import math

import jax
import jax.numpy as jnp
from jax import lax
from jax.experimental import pallas as pl
from jax.experimental.pallas import tpu as pltpu
from jax.sharding import PartitionSpec as P

clip_level = 0.9
MESH = pl.DeviceIdType.MESH
PACK = 4


def legendre_kernel(N, M, c_ref, t_hbm, o_ref, gath, tabs, prod, send, land,
                    tsem, lsem, ssem, rsem, s1, r1, s2, r2):
    Z = N // 2
    Q = c_ref.shape[0]
    L = tabs.shape[1] // PACK
    R = N // M
    me = lax.axis_index("mem")
    mk = lax.axis_index("ma")
    z, p = lax.div(me, 2), lax.rem(me, 2)
    mate = z * 2 + 1 - p

    barrier = pltpu.get_barrier_semaphore()
    for d in range(1, N):
        pl.semaphore_signal(barrier, inc=1, device_id={"mem": lax.rem(me + d, N)}, device_id_type=MESH)
    for d in range(1, M):
        pl.semaphore_signal(barrier, inc=1, device_id={"ma": lax.rem(mk + d, M)}, device_id_type=MESH)

    def table_copy(q):
        return pltpu.make_async_copy(t_hbm.at[q], tabs.at[q], tsem.at[q])

    def own_copy(q):
        return pltpu.make_async_copy(c_ref.at[q], gath.at[q, me], lsem.at[q])

    def hop(way, q, src, ref, dst):
        return pltpu.make_async_remote_copy(
            src_ref=ref, dst_ref=gath.at[q, src], send_sem=ssem.at[way, q, src],
            recv_sem=rsem.at[q, src], device_id={"mem": dst}, device_id_type=MESH)

    pl.semaphore_wait(barrier, N - 1 + M - 1)

    @pl.loop(0, Q)
    def _(q):
        @pl.when(z + 1 < Z)
        def _():
            hop(0, q, me, c_ref.at[q], me + 2).start()

        @pl.when(z > 0)
        def _():
            hop(1, q, me, c_ref.at[q], me - 2).start()

        hop(2, q, me, c_ref.at[q], mate).start()
        own_copy(q).start()
        table_copy(q).start()

    def arrived(q, src):
        hop(2, q, src, gath.at[q, src], mate).wait_recv()

    def relay(q, src, way, more, dst):
        arrived(q, src)

        @pl.when(more)
        def _():
            hop(way, q, src, gath.at[q, src], dst).start()

        hop(2, q, src, gath.at[q, src], mate).start()

    @pl.loop(0, Q + Z - 2)
    def _(s):
        for h in range(1, Z):
            q = s - h + 1
            live = jnp.logical_and(q >= 0, q < Q)

            @pl.when(jnp.logical_and(live, z - h >= 0))
            def _():
                relay(q, me - 2 * h, 0, z + 1 < Z, me + 2)

            @pl.when(jnp.logical_and(live, z + h < Z))
            def _():
                relay(q, me + 2 * h, 1, z > 0, me - 2)

        q = s - (Z - 2)

        @pl.when(q >= 0)
        def _():
            own_copy(q).wait()
            table_copy(q).wait()
            for i in range(Z):
                arrived(q, 2 * i + 1 - p)
            lhs = gath[q].reshape(-1, gath.shape[3])
            full = lax.dot_general(lhs, tabs[q], (((1,), (1,)), ((), ())), preferred_element_type=jnp.float32)
            slot = lax.broadcasted_iota(jnp.int32, (full.shape[0], L), 0) % (2 * PACK) // 2
            diag = full[:, :L]
            for j in range(1, PACK):
                diag = jnp.where(slot == j, full[:, j * L:(j + 1) * L], diag)
            prod[:, :, q] = diag.reshape(prod.shape[0], prod.shape[1], 2 * PACK, L)

    H = send.shape[1]

    def out1(dst):
        return pltpu.make_async_remote_copy(
            src_ref=send.at[dst], dst_ref=land.at[me], send_sem=s1.at[dst],
            recv_sem=r1.at[me], device_id={"mem": dst}, device_id_type=MESH)

    def in1(src):
        return pltpu.make_async_remote_copy(
            src_ref=send.at[src], dst_ref=land.at[src], send_sem=s1.at[src],
            recv_sem=r1.at[src], device_id={"mem": src}, device_id_type=MESH)

    @pl.loop(1, N)
    def _(d):
        dst = lax.rem(me + d, N)
        for h in range(H):
            block = prod[dst * H + h].reshape(-1, L)
            send[dst, h] = block.T.astype(jnp.bfloat16)
        out1(dst).start()

    for h in range(H):
        block = prod[me * H + h].reshape(-1, L)
        land[me, h] = block.T.astype(jnp.bfloat16)

    def out2(kk):
        return pltpu.make_async_remote_copy(
            src_ref=land.at[pl.ds(R * kk, R)], dst_ref=o_ref.at[mk], send_sem=s2.at[kk],
            recv_sem=r2.at[mk], device_id={"ma": kk}, device_id_type=MESH)

    def in2(kk):
        return pltpu.make_async_remote_copy(
            src_ref=land.at[pl.ds(R * kk, R)], dst_ref=o_ref.at[kk], send_sem=s2.at[kk],
            recv_sem=r2.at[kk], device_id={"ma": kk}, device_id_type=MESH)

    def gather_rows(kk):
        for r in range(R):
            src = R * kk + r

            @pl.when(src != me)
            def _():
                in1(src).wait_recv()

    for d in range(1, M):
        kk = lax.rem(mk + d, M)
        gather_rows(kk)
        out2(kk).start()
    gather_rows(mk)
    o_ref[mk] = land[pl.ds(R * mk, R)]
    for d in range(1, M):
        in2(lax.rem(mk + d, M)).wait_recv()

    for d in range(1, M):
        out2(lax.rem(mk + d, M)).wait_send()

    @pl.loop(1, N)
    def _(d):
        out1(lax.rem(me + d, N)).wait_send()

    @pl.loop(0, Q)
    def _(q):
        for i in range(Z):
            src = 2 * i + p
            ref = gath.at[q, src]

            @pl.when(jnp.logical_and(z + 1 < Z, z >= i))
            def _():
                hop(0, q, src, ref, me + 2).wait_send()

            @pl.when(jnp.logical_and(z > 0, z <= i))
            def _():
                hop(1, q, src, ref, me - 2).wait_send()

            hop(2, q, src, ref, mate).wait_send()


def synth_kernel(scale, f_ref, u_ref, v_ref, cb_ref, sb_ref, t_ref, o_ref, lhs, basis):
    step = pl.program_id(0)
    M, R, H, L, W = f_ref.shape
    half = W // 2

    @pl.when(step == 0)
    def _():
        parts = []
        for b in range(2 * H):
            for r in range(R):
                lo = (b % 2) * half
                row = [f_ref[k, r, b // 2].astype(jnp.float32)[:, lo:lo + half] for k in range(M)]
                parts.append(jnp.concatenate(row, axis=1))
        lhs[...] = (jnp.concatenate(parts, axis=0) * scale).astype(jnp.bfloat16) if scale else jnp.concatenate(parts, axis=0).astype(jnp.bfloat16)

    cols = o_ref.shape[2] // 128
    width = u_ref.shape[1]
    shift = lax.rem(width - step * cols, width)
    u = pltpu.roll(u_ref[...], shift, 1)
    v = pltpu.roll(v_ref[...], shift, 1)
    cb, sb = cb_ref[...], sb_ref[...]
    for a in range(cols):
        basis[:, a * 128:(a + 1) * 128] = (u[:, a:a + 1] * cb + v[:, a:a + 1] * sb).astype(jnp.bfloat16)
    pattern = jnp.dot(lhs[...], basis[...], preferred_element_type=jnp.float32)
    pattern = pattern * (1.0 / math.sqrt(basis.shape[0] // 2))
    pattern = jnp.clip(pattern, -clip_level, clip_level).reshape(o_ref.shape)
    o_ref[...] = (t_ref[...].astype(jnp.float32) * (1.0 + pattern)).astype(jnp.bfloat16)


def trig_tables(wavenumber, lon_count):
    rows = jnp.repeat(wavenumber, 2)[:, None]
    odd = (lax.broadcasted_iota(jnp.int32, (rows.shape[0], 1), 0) % 2) == 1
    width = -(-(lon_count // 128) // 128) * 128
    unit = 2.0 * math.pi / lon_count
    coarse = lax.broadcasted_iota(jnp.int32, (1, width), 1)
    fine = lax.broadcasted_iota(jnp.int32, (1, 128), 1)
    far = (rows * 128 % lon_count * coarse % lon_count).astype(jnp.float32) * unit
    near = (rows * fine % lon_count).astype(jnp.float32) * unit
    c, s = jnp.cos(far), jnp.sin(far)
    return jnp.where(odd, -s, c), jnp.where(odd, -c, -s), jnp.cos(near), jnp.sin(near)


def per_device(N, M, ar_state, forcing, ar_decay, amplitude, wavenumber, tables, tendencies):
    members, waves = ar_state.shape[1], ar_state.shape[2]
    degrees = ar_state.shape[4]
    lats = tables.shape[2]
    Q = waves // PACK
    rows = members * 2 * PACK
    owner_index = lax.axis_index("ma")
    own_waves = lax.dynamic_slice_in_dim(wavenumber, owner_index * waves, waves)
    degree_grid = lax.broadcasted_iota(jnp.int32, (waves, degrees), 1)
    kept_mask = (degree_grid >= own_waves[:, None]).astype(jnp.float32)
    updated = (
        ar_decay[:, None, None, None, None] * ar_state + amplitude[:, None, None, None, :] * forcing
    )
    new_state = kept_mask[None, None, :, None, :] * updated
    coefficients = jnp.sum(new_state, axis=0).astype(jnp.bfloat16)
    coefficients = coefficients.reshape(members, Q, 2 * PACK, degrees).transpose(1, 0, 2, 3)
    coefficients = coefficients.reshape(Q, rows, degrees)
    turned = tables.transpose(0, 2, 1).reshape(Q, PACK * lats, degrees)

    H = members // 2
    W = 2 * Q * 2 * PACK
    R = N // M
    any_spec = pl.BlockSpec(memory_space=pl.ANY)
    vmem_spec = pl.BlockSpec(memory_space=pltpu.VMEM)
    fourier = pl.pallas_call(
        functools.partial(legendre_kernel, N, M),
        out_shape=jax.ShapeDtypeStruct((M, R, H, lats, W), jnp.bfloat16),
        in_specs=[vmem_spec, any_spec],
        out_specs=vmem_spec,
        scratch_shapes=[
            pltpu.VMEM((Q, N, rows, degrees), jnp.bfloat16),
            pltpu.VMEM((Q, PACK * lats, degrees), jnp.bfloat16),
            pltpu.VMEM((N * H, 2, Q, 2 * PACK, lats), jnp.float32),
            pltpu.VMEM((N, H, lats, W), jnp.bfloat16),
            pltpu.VMEM((N, H, lats, W), jnp.bfloat16),
            pltpu.SemaphoreType.DMA((Q,)),
            pltpu.SemaphoreType.DMA((Q,)),
            pltpu.SemaphoreType.DMA((3, Q, N)),
            pltpu.SemaphoreType.DMA((Q, N)),
            pltpu.SemaphoreType.DMA((N,)),
            pltpu.SemaphoreType.DMA((N,)),
            pltpu.SemaphoreType.DMA((M,)),
            pltpu.SemaphoreType.DMA((M,)),
        ],
        compiler_params=pltpu.CompilerParams(collective_id=0, has_side_effects=True),
        name="legendre",
    )(coefficients, turned)

    lons = tendencies.shape[2]
    u, v, cb, sb = trig_tables(wavenumber, lons)
    tile = 512
    whole = lambda x: pl.BlockSpec(x.shape, lambda i: (0,) * x.ndim)
    grid_spec = pl.BlockSpec((tendencies.shape[0], tendencies.shape[1], tile), lambda i: (0, 0, i))
    perturbed = pl.pallas_call(
        functools.partial(synth_kernel, None),
        grid=(lons // tile,),
        out_shape=jax.ShapeDtypeStruct(tendencies.shape, jnp.bfloat16),
        in_specs=[whole(fourier), whole(u), whole(v), whole(cb), whole(sb), grid_spec],
        out_specs=grid_spec,
        scratch_shapes=[
            pltpu.VMEM((tendencies.shape[0] * tendencies.shape[1], u.shape[0]), jnp.bfloat16),
            pltpu.VMEM((u.shape[0], tile), jnp.bfloat16),
        ],
        name="synthesis",
    )(fourier, u, v, cb, sb, tendencies)
    return (perturbed, new_state)


def solution(mesh):
    return jax.shard_map(
        functools.partial(per_device, mesh.shape["mem"], mesh.shape["ma"]),
        mesh=mesh,
        in_specs=(
            P(None, "mem", "ma", None, None),
            P(None, "mem", "ma", None, None),
            P(),
            P(),
            P(),
            P("ma", None, "mem"),
            P("mem", "ma", None),
        ),
        out_specs=(P("mem", "ma", None), P(None, "mem", "ma", None, None)),
        check_vma=False,
    )
```

time: 145 us -> 91.3 us (0.63)
  Pallas kernels: 0 us -> 75.3 us
  waiting for transfers between devices: 58.9 us -> 0 us
  local copies, waits for them, and re-layouts: 28.3 us -> 3.02 us
  other arithmetic: 26.9 us -> 11.8 us
  between operations: 14.1 us -> 0.67 us
  matrix products: 9.07 us -> 0 us
  starting transfers between devices: 7.25 us -> 0 us
    pallas_call x0 -> x2, Pallas kernels: none -> 75.3 us  [the longest x1 64.2 us: per_device(): pl.pallas_call(functools.partial(legendre_kernel, N, M), out_shape=jax.Sh...]
    all_gather x1 -> x0, waiting for transfers between devices: 58.8 us -> none  [per_device(): everyone = lax.all_gather(coefficients, 'mem', axis=0, tiled=True)]
    another operation x2 -> x0, other arithmetic: 15 us -> none
    dot_general x2 -> x0, matrix products: 9.07 us -> none  [the longest x1 5.56 us: per_device(): jnp.einsum('bmcn,mnl->blmc', everyone, tables, preferred_element_type=jnp...]
    convert_element_type x2 -> x0, local copies, waits for them, and re-layouts: 7.82 us -> none  [the longest x1 6.47 us: basis_table(): stacked.reshape(2 * wavenumber.shape[0], lon_count).astype(jnp.bfloat16)]
    unnamed x10 -> x0, local copies, waits for them, and re-layouts: 7.6 us -> none
    all_to_all x2 -> x0, starting transfers between devices: 7.21 us -> none  [the longest x1 3.65 us: per_device(): lax.all_to_all(lax.all_to_all(fourier, 'mem', split_axis=0, concat_axis=1...]
    all_to_all x3 -> x0, local copies, waits for them, and re-layouts: 6.08 us -> none  [the longest x2 4.56 us: per_device(): lax.all_to_all(fourier, 'mem', split_axis=0, concat_axis=1, tiled=True)]
  transfers between devices with their start and end apart: 3 -> 0, of which waited for: 1 -> 0; matrix products, arithmetic and copies ran while one was open for 18% -> 0% of each run, Pallas kernels for 0% -> 0%
where the time goes in v1:
time: 91.3 us; the launch traced here: 90.9 us
  Pallas kernels  75.3 us (82%)
  other arithmetic  11.8 us (13%)
  local copies, waits for them, and re-layouts  3.02 us (3%)
    pallas_call x1, Pallas kernels, per_device(): pl.pallas_call(functools.partial(legendre_kernel, N, M), out_shape=jax.Sh...  64.2 us
    pallas_call x1, Pallas kernels, per_device(): pl.pallas_call(functools.partial(synth_kernel, None), grid=(lons // tile,...  11.1 us
    reduce_sum x1, other arithmetic, per_device(): coefficients = jnp.sum(new_state, axis=0).astype(jnp.bfloat16)  9.09 us

profile of v1, /device:TPU:0, one launch (start us, length us, event | category | flops | bytes accessed | tf_op | source)
XLA Modules:
  0.0 90.9 jit_solution(5867013344704555420)
XLA Ops:
  0.6 0.7 dynamic_slice.3
  1.4 0.7 broadcast_in_dim.21
  2.1 0.1 broadcast_in_dim_reshape.3
  2.3 0.1 fusion
  2.4 1.3 %negate_select_fusion = (f32[256,128]{1,0:T(8,128)}, f32[256,128]{1,0:T(8,128)}) fusion(s32[256]{0:T(256)S(1)} %and_select_fusion, pred[256]{0:T(512)(128)(4,1)S(1)} %fusion.15), kind=kLoop, calls=%fused_computation.15 | loop fusion | flops 425984 | bytes 263424 | tf_op jit(solution)/shard_map/jit(_where)/select_n | solution.py:216
  3.7 1.3 %fusion.7 = (f32[256,128]{1,0:T(8,128)}, f32[256,128]{1,0:T(8,128)}) fusion(s32[256]{0:T(256)S(1)} %broadcast_in_dim_reshape.3), kind=kLoop, calls=%fused_computation.13 | loop fusion | flops 294912 | bytes 263168 | tf_op jit(solution)/shard_map/sin | solution.py:216
  5.0 9.1 %fusion.16 = (bf16[4,32,2,1280]{3,2,1,0:T(2,128)(2,1)S(1)}, f32[3,4,32,2,1280]{4,3,2,1,0:T(2,128)}) fusion(f32[3,4,32,2,1280]{4,3,2,1,0:T(2,128)} %param.8, f32[3,1280]{1,0:T(4,128)} %param.10, f32[3,4,32,2,1280]{4,3,2,1,0:T(2,128)} %param.7, f32[3]{0:T(128)} %param.9, f32[32,1280]{1,0:T(8,128)S(1)} %fusion), kind=kLoop, calls=%fused_computation.27 | loop fusion | flops 4587520 | bytes 12631052 | tf_op jit(solution)/shard_map/reduce_sum | solution.py:233
  14.1 0.5 copy.10
  14.6 0.9 copy.13
  15.5 64.2 %legendre.1.f_ref = bf16[4,2,2,40,128]{4,3,2,1,0:T(8,128)(2,1)} custom-call(bf16[8,32,1280]{2,1,0:T(8,128)(2,1)} %bitcast.10, bf16[8,160,1280]{2,1,0:T(8,128)(2,1)} %bitcast.9), custom_call_target="tpu_custom_call" | custom-call | tf_op jit(solution)/shard_map/legendre/pallas_call | solution.py:243
  79.8 11.1 %synthesis.1 = bf16[4,80,5120]{2,1,0:T(8,128)(2,1)} custom-call(bf16[4,2,2,40,128]{4,3,2,1,0:T(8,128)(2,1)} %legendre.1.f_ref, f32[256,128]{1,0:T(8,128)} %get-tuple-element.5.u_ref, f32[256,128]{1,0:T(8,128)} %get-tuple-element.4.v_ref, f32[256,128]{1,0:T(8,128)} %get-tuple-element.7.cb_ref, f32[256,128]{1,0:T(8,128)} %get-tuple-element.6.sb_ref, ...), custom_call_target="tpu_custom_call" | custom-call | tf_op jit(solution)/shard_map/synthesis/pallas_call | solution.py:272
  (2 shorter events, 0.0 us)

commit v2 on v1

--- a/solution.py
+++ b/solution.py
@@ -13,8 +13,8 @@
 PACK = 4
 
 
-def legendre_kernel(N, M, c_ref, t_hbm, o_ref, gath, tabs, prod, send, land,
-                    tsem, lsem, ssem, rsem, s1, r1, s2, r2):
+def legendre_kernel(N, M, c_ref, t_hbm, u_ref, v_ref, cb_ref, sb_ref, o_ref, basis_hbm, basis, gath, tabs, prod, send, land,
+                    bsem, tsem, lsem, ssem, rsem, s1, r1, s2, r2):
     Z = N // 2
     Q = c_ref.shape[0]
     L = tabs.shape[1] // PACK
@@ -69,8 +69,23 @@
 
         hop(2, q, src, gath.at[q, src], mate).start()
 
-    @pl.loop(0, Q + Z - 2)
+    steps = Q + Z - 2
+    cols = basis.shape[2] // 128
+
+    def basis_copy(s):
+        return pltpu.make_async_copy(
+            basis.at[s], basis_hbm.at[:, pl.ds(s * cols * 128, cols * 128)], bsem.at[s])
+
+    @pl.loop(0, steps)
     def _(s):
+        width = u_ref.shape[1]
+        turn = lax.rem(width - s * cols, width)
+        u = pltpu.roll(u_ref[...], turn, 1)
+        v = pltpu.roll(v_ref[...], turn, 1)
+        for a in range(cols):
+            value = u[:, a:a + 1] * cb_ref[...] + v[:, a:a + 1] * sb_ref[...]
+            basis[s, :, a * 128:(a + 1) * 128] = value.astype(jnp.bfloat16)
+        basis_copy(s).start()
         for h in range(1, Z):
             q = s - h + 1
             live = jnp.logical_and(q >= 0, q < Q)
@@ -93,7 +108,7 @@
                 arrived(q, 2 * i + 1 - p)
             lhs = gath[q].reshape(-1, gath.shape[3])
             full = lax.dot_general(lhs, tabs[q], (((1,), (1,)), ((), ())), preferred_element_type=jnp.float32)
-            slot = lax.broadcasted_iota(jnp.int32, (full.shape[0], L), 0) % (2 * PACK) // 2
+            slot = lax.broadcasted_iota(jnp.int32, (full.shape[0], L), 0) // 2 % PACK
             diag = full[:, :L]
             for j in range(1, PACK):
                 diag = jnp.where(slot == j, full[:, j * L:(j + 1) * L], diag)
@@ -150,6 +165,10 @@
     for d in range(1, M):
         in2(lax.rem(mk + d, M)).wait_recv()
 
+    @pl.loop(0, steps)
+    def _(s):
+        basis_copy(s).wait()
+
     for d in range(1, M):
         out2(lax.rem(mk + d, M)).wait_send()
 
@@ -174,12 +193,54 @@
             hop(2, q, src, ref, mate).wait_send()
 
 
-def synth_kernel(scale, f_ref, u_ref, v_ref, cb_ref, sb_ref, t_ref, o_ref, lhs, basis):
+def update_kernel(m_ref, d_ref, amp_ref, s_ref, f_ref, n_ref, c_ref, u_ref, v_ref, cb_ref, sb_ref, total, lons):
     step = pl.program_id(0)
+    scales, members, _, _, degrees = s_ref.shape
+    first = lax.axis_index("ma") * (pl.num_programs(0) * PACK) + step * PACK
+    degree = lax.broadcasted_iota(jnp.int32, (2, degrees), 1)
+    for j in range(PACK):
+        kept = jnp.where(degree >= m_ref[first + j], 1.0, 0.0).astype(jnp.float32)
+        for b in range(members):
+            acc = None
+            for i in range(scales):
+                new = kept * (d_ref[i] * s_ref[i, b, j] + amp_ref[i:i + 1, :] * f_ref[i, b, j])
+                n_ref[i, b, j] = new
+                acc = new if acc is None else acc + new
+            total[b * 2 * PACK + 2 * j:b * 2 * PACK + 2 * j + 2, :] = acc
+    c_ref[0] = total[...].astype(jnp.bfloat16)
+
+    unit = 2.0 * math.pi / lons
+    width = u_ref.shape[1]
+    group = lax.broadcasted_iota(jnp.int32, (8, 1), 0)
+    shift = (group % 2).astype(jnp.float32) * (lons // 4)
+
+    def angle(x):
+        return (x - lons * jnp.floor(x * (1.0 / lons))) * unit
+
+    for g in range(u_ref.shape[0] // 8):
+        at = (step * (u_ref.shape[0] // 8) + g) * PACK
+        m = m_ref[at]
+        near = jnp.full((8, 128), m, jnp.int32)
+        far = jnp.full((8, width), lax.rem(m * 128, lons), jnp.int32)
+        for j in range(1, PACK):
+            m = m_ref[at + j]
+            near = jnp.where(group // 2 == j, m, near)
+            far = jnp.where(group // 2 == j, lax.rem(m * 128, lons), far)
+        near = near * lax.broadcasted_iota(jnp.int32, (8, 128), 1)
+        far = far * lax.broadcasted_iota(jnp.int32, (8, width), 1)
+        near = angle(near.astype(jnp.float32))
+        far = angle(far.astype(jnp.float32) + shift)
+        u_ref[g * 8:(g + 1) * 8] = jnp.cos(far)
+        v_ref[g * 8:(g + 1) * 8] = -jnp.sin(far)
+        cb_ref[g * 8:(g + 1) * 8] = jnp.cos(near)
+        sb_ref[g * 8:(g + 1) * 8] = jnp.sin(near)
+
+
+def synth_kernel(f_ref, basis_ref, t_ref, o_ref, lhs):
     M, R, H, L, W = f_ref.shape
     half = W // 2
 
-    @pl.when(step == 0)
+    @pl.when(pl.program_id(0) == 0)
     def _():
         parts = []
         for b in range(2 * H):
@@ -187,33 +248,12 @@
                 lo = (b % 2) * half
                 row = [f_ref[k, r, b // 2].astype(jnp.float32)[:, lo:lo + half] for k in range(M)]
                 parts.append(jnp.concatenate(row, axis=1))
-        lhs[...] = (jnp.concatenate(parts, axis=0) * scale).astype(jnp.bfloat16) if scale else jnp.concatenate(parts, axis=0).astype(jnp.bfloat16)
-
-    cols = o_ref.shape[2] // 128
-    width = u_ref.shape[1]
-    shift = lax.rem(width - step * cols, width)
-    u = pltpu.roll(u_ref[...], shift, 1)
-    v = pltpu.roll(v_ref[...], shift, 1)
-    cb, sb = cb_ref[...], sb_ref[...]
-    for a in range(cols):
-        basis[:, a * 128:(a + 1) * 128] = (u[:, a:a + 1] * cb + v[:, a:a + 1] * sb).astype(jnp.bfloat16)
-    pattern = jnp.dot(lhs[...], basis[...], preferred_element_type=jnp.float32)
-    pattern = pattern * (1.0 / math.sqrt(basis.shape[0] // 2))
-    pattern = jnp.clip(pattern, -clip_level, clip_level).reshape(o_ref.shape)
-    o_ref[...] = (t_ref[...].astype(jnp.float32) * (1.0 + pattern)).astype(jnp.bfloat16)
-
-
-def trig_tables(wavenumber, lon_count):
-    rows = jnp.repeat(wavenumber, 2)[:, None]
-    odd = (lax.broadcasted_iota(jnp.int32, (rows.shape[0], 1), 0) % 2) == 1
-    width = -(-(lon_count // 128) // 128) * 128
-    unit = 2.0 * math.pi / lon_count
-    coarse = lax.broadcasted_iota(jnp.int32, (1, width), 1)
-    fine = lax.broadcasted_iota(jnp.int32, (1, 128), 1)
-    far = (rows * 128 % lon_count * coarse % lon_count).astype(jnp.float32) * unit
-    near = (rows * fine % lon_count).astype(jnp.float32) * unit
-    c, s = jnp.cos(far), jnp.sin(far)
-    return jnp.where(odd, -s, c), jnp.where(odd, -c, -s), jnp.cos(near), jnp.sin(near)
+        lhs[...] = jnp.concatenate(parts, axis=0).astype(jnp.bfloat16)
+
+    pattern = jnp.dot(lhs[...], basis_ref[...], preferred_element_type=jnp.float32)
+    scale = 1.0 / math.sqrt(basis_ref.shape[0] // 2)
+    factor = jnp.clip(pattern * scale + 1.0, 1.0 - clip_level, 1.0 + clip_level)
+    o_ref[...] = (t_ref[...].astype(jnp.float32) * factor.reshape(o_ref.shape)).astype(jnp.bfloat16)
 
 
 def per_device(N, M, ar_state, forcing, ar_decay, amplitude, wavenumber, tables, tendencies):
@@ -222,17 +262,28 @@
     lats = tables.shape[2]
     Q = waves // PACK
     rows = members * 2 * PACK
-    owner_index = lax.axis_index("ma")
-    own_waves = lax.dynamic_slice_in_dim(wavenumber, owner_index * waves, waves)
-    degree_grid = lax.broadcasted_iota(jnp.int32, (waves, degrees), 1)
-    kept_mask = (degree_grid >= own_waves[:, None]).astype(jnp.float32)
-    updated = (
-        ar_decay[:, None, None, None, None] * ar_state + amplitude[:, None, None, None, :] * forcing
-    )
-    new_state = kept_mask[None, None, :, None, :] * updated
-    coefficients = jnp.sum(new_state, axis=0).astype(jnp.bfloat16)
-    coefficients = coefficients.reshape(members, Q, 2 * PACK, degrees).transpose(1, 0, 2, 3)
-    coefficients = coefficients.reshape(Q, rows, degrees)
+    scales = ar_state.shape[0]
+    lons = tendencies.shape[2]
+    modes = 2 * wavenumber.shape[0]
+    width = -(-(lons // 128) // 128) * 128
+    state_spec = pl.BlockSpec((scales, members, PACK, 2, degrees), lambda i: (0, 0, i, 0, 0))
+    smem = pl.BlockSpec(memory_space=pltpu.SMEM)
+    trig = lambda w: (pl.BlockSpec((modes // Q, w), lambda i: (i, 0)), jax.ShapeDtypeStruct((modes, w), jnp.float32))
+    tables_out = [trig(width), trig(width), trig(128), trig(128)]
+    new_state, coefficients, u, v, cb, sb = pl.pallas_call(
+        functools.partial(update_kernel, lons=lons),
+        grid=(Q,),
+        out_shape=[
+            jax.ShapeDtypeStruct(ar_state.shape, jnp.float32),
+            jax.ShapeDtypeStruct((Q, rows, degrees), jnp.bfloat16),
+        ] + [x[1] for x in tables_out],
+        in_specs=[smem, smem, pl.BlockSpec(amplitude.shape, lambda i: (0, 0)), state_spec, state_spec],
+        out_specs=[state_spec, pl.BlockSpec((1, rows, degrees), lambda i: (i, 0, 0))] + [x[0] for x in tables_out],
+        scratch_shapes=[
+            pltpu.VMEM((rows, degrees), jnp.float32),
+        ],
+        name="update",
+    )(wavenumber, ar_decay, amplitude, ar_state, forcing)
     turned = tables.transpose(0, 2, 1).reshape(Q, PACK * lats, degrees)
 
     H = members // 2
@@ -240,17 +291,24 @@
     R = N // M
     any_spec = pl.BlockSpec(memory_space=pl.ANY)
     vmem_spec = pl.BlockSpec(memory_space=pltpu.VMEM)
-    fourier = pl.pallas_call(
+    steps = Q + N // 2 - 2
+    cols = lons // 128 // steps
+    fourier, basis = pl.pallas_call(
         functools.partial(legendre_kernel, N, M),
-        out_shape=jax.ShapeDtypeStruct((M, R, H, lats, W), jnp.bfloat16),
-        in_specs=[vmem_spec, any_spec],
-        out_specs=vmem_spec,
+        out_shape=[
+            jax.ShapeDtypeStruct((M, R, H, lats, W), jnp.bfloat16),
+            jax.ShapeDtypeStruct((modes, lons), jnp.bfloat16),
+        ],
+        in_specs=[vmem_spec, any_spec] + [vmem_spec] * 4,
+        out_specs=[vmem_spec, any_spec],
         scratch_shapes=[
+            pltpu.VMEM((steps, modes, cols * 128), jnp.bfloat16),
             pltpu.VMEM((Q, N, rows, degrees), jnp.bfloat16),
             pltpu.VMEM((Q, PACK * lats, degrees), jnp.bfloat16),
             pltpu.VMEM((N * H, 2, Q, 2 * PACK, lats), jnp.float32),
             pltpu.VMEM((N, H, lats, W), jnp.bfloat16),
             pltpu.VMEM((N, H, lats, W), jnp.bfloat16),
+            pltpu.SemaphoreType.DMA((steps,)),
             pltpu.SemaphoreType.DMA((Q,)),
             pltpu.SemaphoreType.DMA((Q,)),
             pltpu.SemaphoreType.DMA((3, Q, N)),
@@ -262,25 +320,23 @@
         ],
         compiler_params=pltpu.CompilerParams(collective_id=0, has_side_effects=True),
         name="legendre",
-    )(coefficients, turned)
-
-    lons = tendencies.shape[2]
-    u, v, cb, sb = trig_tables(wavenumber, lons)
-    tile = 512
-    whole = lambda x: pl.BlockSpec(x.shape, lambda i: (0,) * x.ndim)
+    )(coefficients, turned, u, v, cb, sb)
+
+    tile = lons // 5
     grid_spec = pl.BlockSpec((tendencies.shape[0], tendencies.shape[1], tile), lambda i: (0, 0, i))
     perturbed = pl.pallas_call(
-        functools.partial(synth_kernel, None),
+        synth_kernel,
         grid=(lons // tile,),
         out_shape=jax.ShapeDtypeStruct(tendencies.shape, jnp.bfloat16),
-        in_specs=[whole(fourier), whole(u), whole(v), whole(cb), whole(sb), grid_spec],
+        in_specs=[
+            pl.BlockSpec(fourier.shape, lambda i: (0,) * 5),
+            pl.BlockSpec((modes, tile), lambda i: (0, i)),
+            grid_spec,
+        ],
         out_specs=grid_spec,
-        scratch_shapes=[
-            pltpu.VMEM((tendencies.shape[0] * tendencies.shape[1], u.shape[0]), jnp.bfloat16),
-            pltpu.VMEM((u.shape[0], tile), jnp.bfloat16),
-        ],
+        scratch_shapes=[pltpu.VMEM((tendencies.shape[0] * tendencies.shape[1], modes), jnp.bfloat16)],
         name="synthesis",
-    )(fourier, u, v, cb, sb, tendencies)
+    )(fourier, basis, tendencies)
     return (perturbed, new_state)
 
 

time: 91.3 us -> 83.3 us (0.912)
  other arithmetic: 11.8 us -> 0 us
  Pallas kernels: 75.3 us -> 82.2 us
  local copies, waits for them, and re-layouts: 3.02 us -> 0 us
    reduce_sum x1 -> x0, other arithmetic: 9.09 us -> none  [per_device(): coefficients = jnp.sum(new_state, axis=0).astype(jnp.bfloat16)]
    pallas_call x2 -> x3, Pallas kernels: 75.3 us -> 82.2 us  [the longest x1 65 us: per_device(): pl.pallas_call(functools.partial(legendre_kernel, N, M), out_shape=[jax.S...]
    select_n x2 -> x0, other arithmetic: 1.36 us -> none  [the longest x1 1.34 us: trig_tables(): jnp.where(odd, -c, -s)]
    sin x1 -> x0, other arithmetic: 1.32 us -> none  [trig_tables(): jnp.sin(near)]
where the time goes in v2:
time: 83.3 us; the launch traced here: 82.9 us
  Pallas kernels  82.2 us (99%)
    pallas_call x1, Pallas kernels, per_device(): pl.pallas_call(functools.partial(legendre_kernel, N, M), out_shape=[jax.S...  65 us
    pallas_call x1, Pallas kernels, per_device(): pl.pallas_call(functools.partial(update_kernel, lons=lons), grid=(Q,), ou...  10.1 us
    pallas_call x1, Pallas kernels, per_device(): pl.pallas_call(synth_kernel, grid=(lons // tile,), out_shape=jax.ShapeDty...  7.09 us

profile of v2, /device:TPU:0, one launch (start us, length us, event | category | flops | bytes accessed | tf_op | source)
XLA Modules:
  0.0 82.9 jit_solution(1035999054468973663)
XLA Ops:
  0.6 10.1 %update.1 = (f32[3,4,32,2,1280]{4,3,2,1,0:T(2,128)}, bf16[8,32,1280]{2,1,0:T(8,128)(2,1)}, f32[256,128]{1,0:T(8,128)}, f32[256,128]{1,0:T(8,128)}, f32[256,128]{1,0:T(8,128)}, /*index=5*/f32[256,128]{1,0:T(8,128)}) custom-call(s32[128]{0:T(128)} %m_ref.1, f32[3]{0:T(128)} %d_ref.1, f32[3,1280]{1,0:T(4,128)} %amp_ref.1, f32[3,4,32,2,1280]{4,3,2,1,0:T(2,128)} %s_ref.1, ...), custom_call_target="tpu_custom_call" | custom-call | tf_op jit(solution)/shard_map/update/pallas_call | solution.py:273
  10.8 65.0 %legendre.1 = (bf16[4,2,2,40,128]{4,3,2,1,0:T(8,128)(2,1)}, bf16[256,5120]{1,0:T(8,128)(2,1)}) custom-call(bf16[8,32,1280]{2,1,0:T(8,128)(2,1)} %get-tuple-element.10.c_ref, bf16[8,160,1280]{2,1,0:T(8,128)(2,1)} %bitcast.3, f32[256,128]{1,0:T(8,128)} %get-tuple-element.11.u_ref, f32[256,128]{1,0:T(8,128)} %get-tuple-element.12.v_ref, ...), custom_call_target="tpu_custom_call" | custom-call | tf_op jit(solution)/shard_map/legendre/pallas_call | solution.py:296
  75.8 7.1 %synthesis.1 = bf16[4,80,5120]{2,1,0:T(8,128)(2,1)} custom-call(bf16[4,2,2,40,128]{4,3,2,1,0:T(8,128)(2,1)} %get-tuple-element.15.f_ref, bf16[256,5120]{1,0:T(8,128)(2,1)} %get-tuple-element.16.basis_ref, bf16[4,80,5120]{2,1,0:T(8,128)(2,1)} %t_ref.1), custom_call_target="tpu_custom_call" | custom-call | tf_op jit(solution)/shard_map/synthesis/pallas_call | solution.py:327

commit v3 on v2

--- a/solution.py
+++ b/solution.py
@@ -13,8 +13,13 @@
 PACK = 4
 
 
+def tail_chunks(chunks, chips):
+    return chunks // 4 if chips >= 4 else 0
+
+
 def legendre_kernel(N, M, c_ref, t_hbm, u_ref, v_ref, cb_ref, sb_ref, o_ref, basis_hbm, basis, gath, tabs, prod, send, land,
-                    bsem, tsem, lsem, ssem, rsem, s1, r1, s2, r2):
+                    adopt, prod2, send2, land2,
+                    bsem, tsem, lsem, ssem, rsem, s1, r1, s2, r2, asend, arecv, s1b, r1b):
     Z = N // 2
     Q = c_ref.shape[0]
     L = tabs.shape[1] // PACK
@@ -23,6 +28,20 @@
     mk = lax.axis_index("ma")
     z, p = lax.div(me, 2), lax.rem(me, 2)
     mate = z * 2 + 1 - p
+    E = tail_chunks(Q, Z)
+    end = jnp.logical_or(z == 0, z == Z - 1)
+    adopter = jnp.logical_or(z == 1, z == Z - 2)
+    inner = jnp.where(z == 0, me + 2, me - 2)
+    corner = p + jnp.where(z == Z - 2, 2, 0)
+
+    def here(q):
+        return jnp.logical_not(jnp.logical_and(end, q >= Q - E))
+
+    def goes_up(q):
+        return jnp.logical_and(z + 1 < Z, jnp.logical_not(jnp.logical_and(z == Z - 2, q >= Q - E)))
+
+    def goes_down(q):
+        return jnp.logical_and(z > 0, jnp.logical_not(jnp.logical_and(z == 1, q >= Q - E)))
 
     barrier = pltpu.get_barrier_semaphore()
     for d in range(1, N):
@@ -45,17 +64,31 @@
 
     @pl.loop(0, Q)
     def _(q):
-        @pl.when(z + 1 < Z)
+        @pl.when(goes_up(q))
         def _():
             hop(0, q, me, c_ref.at[q], me + 2).start()
 
-        @pl.when(z > 0)
+        @pl.when(goes_down(q))
         def _():
             hop(1, q, me, c_ref.at[q], me - 2).start()
 
-        hop(2, q, me, c_ref.at[q], mate).start()
-        own_copy(q).start()
+        @pl.when(here(q))
+        def _():
+            hop(2, q, me, c_ref.at[q], mate).start()
+            own_copy(q).start()
+
         table_copy(q).start()
+
+    def adopt_copy(e):
+        return pltpu.make_async_remote_copy(
+            src_ref=tabs.at[Q - E + e], dst_ref=adopt.at[e], send_sem=asend.at[e],
+            recv_sem=arecv.at[e], device_id={"mem": inner}, device_id_type=MESH)
+
+    for e in range(E):
+        @pl.when(end)
+        def _():
+            table_copy(Q - E + e).wait()
+            adopt_copy(e).start()
 
     def arrived(q, src):
         hop(2, q, src, gath.at[q, src], mate).wait_recv()
@@ -90,29 +123,45 @@
             q = s - h + 1
             live = jnp.logical_and(q >= 0, q < Q)
 
+            live = jnp.logical_and(live, here(q))
+
             @pl.when(jnp.logical_and(live, z - h >= 0))
             def _():
-                relay(q, me - 2 * h, 0, z + 1 < Z, me + 2)
+                relay(q, me - 2 * h, 0, goes_up(q), me + 2)
 
             @pl.when(jnp.logical_and(live, z + h < Z))
             def _():
-                relay(q, me + 2 * h, 1, z > 0, me - 2)
+                relay(q, me + 2 * h, 1, goes_down(q), me - 2)
 
         q = s - (Z - 2)
 
-        @pl.when(q >= 0)
+        def rows_of(table):
+            lhs = gath[q].reshape(-1, gath.shape[3])
+            full = lax.dot_general(lhs, table, (((1,), (1,)), ((), ())), preferred_element_type=jnp.float32)
+            slot = lax.broadcasted_iota(jnp.int32, (full.shape[0], L), 0) // 2 % PACK
+            diag = full[:, :L]
+            for j in range(1, PACK):
+                diag = jnp.where(slot == j, full[:, j * L:(j + 1) * L], diag)
+            return diag.reshape(prod.shape[0], prod.shape[1], 2 * PACK, L)
+
+        @pl.when(jnp.logical_and(q >= 0, here(q)))
         def _():
             own_copy(q).wait()
             table_copy(q).wait()
             for i in range(Z):
                 arrived(q, 2 * i + 1 - p)
-            lhs = gath[q].reshape(-1, gath.shape[3])
-            full = lax.dot_general(lhs, tabs[q], (((1,), (1,)), ((), ())), preferred_element_type=jnp.float32)
-            slot = lax.broadcasted_iota(jnp.int32, (full.shape[0], L), 0) // 2 % PACK
-            diag = full[:, :L]
-            for j in range(1, PACK):
-                diag = jnp.where(slot == j, full[:, j * L:(j + 1) * L], diag)
-            prod[:, :, q] = diag.reshape(prod.shape[0], prod.shape[1], 2 * PACK, L)
+            prod[:, :, q] = rows_of(tabs[q])
+
+        if E:
+            @pl.when(jnp.logical_not(here(q)))
+            def _():
+                prod[:, :, q] = jnp.zeros((prod.shape[0], prod.shape[1], 2 * PACK, L), jnp.float32)
+
+            @pl.when(jnp.logical_and(adopter, q >= Q - E))
+            def _():
+                e = q - (Q - E)
+                adopt_copy(e).wait_recv()
+                prod2[:, :, e] = rows_of(adopt[e])
 
     H = send.shape[1]
 
@@ -138,6 +187,34 @@
         block = prod[me * H + h].reshape(-1, L)
         land[me, h] = block.T.astype(jnp.bfloat16)
 
+    def out1b(dst):
+        return pltpu.make_async_remote_copy(
+            src_ref=send2.at[dst], dst_ref=land2.at[corner], send_sem=s1b.at[dst],
+            recv_sem=r1b.at[corner], device_id={"mem": dst}, device_id_type=MESH)
+
+    def in1b(e, src):
+        return pltpu.make_async_remote_copy(
+            src_ref=send2.at[src], dst_ref=land2.at[e], send_sem=s1b.at[src],
+            recv_sem=r1b.at[e], device_id={"mem": src}, device_id_type=MESH)
+
+    def spare_rows(dst, h):
+        at = dst * H + h
+        block = jnp.concatenate([prod[at][:, :Q - E], prod2[at]], axis=1).reshape(-1, L)
+        return block.T.astype(jnp.bfloat16)
+
+    if E:
+        @pl.when(adopter)
+        def _():
+            @pl.loop(1, N)
+            def _(d):
+                dst = lax.rem(me + d, N)
+                for h in range(H):
+                    send2[dst, h] = spare_rows(dst, h)
+                out1b(dst).start()
+
+            for h in range(H):
+                land2[corner, h] = spare_rows(me, h)
+
     def out2(kk):
         return pltpu.make_async_remote_copy(
             src_ref=land.at[pl.ds(R * kk, R)], dst_ref=o_ref.at[mk], send_sem=s2.at[kk],
@@ -155,6 +232,24 @@
             @pl.when(src != me)
             def _():
                 in1(src).wait_recv()
+
+            if E:
+                low, high = src < 2, src >= N - 2
+                helper = jnp.where(low, src + 2, src - 2)
+                e = lax.rem(src, 2) + jnp.where(high, 2, 0)
+
+                @pl.when(jnp.logical_and(jnp.logical_or(low, high), helper != me))
+                def _():
+                    in1b(e, helper).wait_recv()
+
+                @pl.when(jnp.logical_or(low, high))
+                def _():
+                    lane = lax.broadcasted_iota(jnp.int32, land.shape[2:], 1)
+                    spare = lane % (2 * PACK * Q) >= 2 * PACK * (Q - E)
+                    for h in range(H):
+                        own = land[src, h].astype(jnp.float32)
+                        other = land2[e, h].astype(jnp.float32)
+                        land[src, h] = jnp.where(spare, other, own).astype(jnp.bfloat16)
 
     for d in range(1, M):
         kk = lax.rem(mk + d, M)
@@ -182,15 +277,29 @@
             src = 2 * i + p
             ref = gath.at[q, src]
 
-            @pl.when(jnp.logical_and(z + 1 < Z, z >= i))
+            @pl.when(jnp.logical_and(goes_up(q), z >= i))
             def _():
                 hop(0, q, src, ref, me + 2).wait_send()
 
-            @pl.when(jnp.logical_and(z > 0, z <= i))
+            @pl.when(jnp.logical_and(goes_down(q), z <= i))
             def _():
                 hop(1, q, src, ref, me - 2).wait_send()
 
-            hop(2, q, src, ref, mate).wait_send()
+            @pl.when(here(q))
+            def _():
+                hop(2, q, src, ref, mate).wait_send()
+
+    if E:
+        @pl.when(end)
+        def _():
+            for e in range(E):
+                adopt_copy(e).wait_send()
+
+        @pl.when(adopter)
+        def _():
+            @pl.loop(1, N)
+            def _(d):
+                out1b(lax.rem(me + d, N)).wait_send()
 
 
 def update_kernel(m_ref, d_ref, amp_ref, s_ref, f_ref, n_ref, c_ref, u_ref, v_ref, cb_ref, sb_ref, total, lons):
@@ -292,6 +401,7 @@
     any_spec = pl.BlockSpec(memory_space=pl.ANY)
     vmem_spec = pl.BlockSpec(memory_space=pltpu.VMEM)
     steps = Q + N // 2 - 2
+    spare = max(tail_chunks(Q, N // 2), 1)
     cols = lons // 128 // steps
     fourier, basis = pl.pallas_call(
         functools.partial(legendre_kernel, N, M),
@@ -308,6 +418,10 @@
             pltpu.VMEM((N * H, 2, Q, 2 * PACK, lats), jnp.float32),
             pltpu.VMEM((N, H, lats, W), jnp.bfloat16),
             pltpu.VMEM((N, H, lats, W), jnp.bfloat16),
+            pltpu.VMEM((spare, PACK * lats, degrees), jnp.bfloat16),
+            pltpu.VMEM((N * H, 2, spare, 2 * PACK, lats), jnp.float32),
+            pltpu.VMEM((N, H, lats, W), jnp.bfloat16),
+            pltpu.VMEM((4, H, lats, W), jnp.bfloat16),
             pltpu.SemaphoreType.DMA((steps,)),
             pltpu.SemaphoreType.DMA((Q,)),
             pltpu.SemaphoreType.DMA((Q,)),
@@ -317,6 +431,10 @@
             pltpu.SemaphoreType.DMA((N,)),
             pltpu.SemaphoreType.DMA((M,)),
             pltpu.SemaphoreType.DMA((M,)),
+            pltpu.SemaphoreType.DMA((spare,)),
+            pltpu.SemaphoreType.DMA((spare,)),
+            pltpu.SemaphoreType.DMA((N,)),
+            pltpu.SemaphoreType.DMA((4,)),
         ],
         compiler_params=pltpu.CompilerParams(collective_id=0, has_side_effects=True),
         name="legendre",

time: 83.3 us -> 76.6 us (0.920)
  Pallas kernels: 82.2 us -> 75.5 us
    pallas_call x1, Pallas kernels: 65 us -> 58.3 us  [per_device(): pl.pallas_call(functools.partial(legendre_kernel, N, M), out_shape=[jax.S...]
where the time goes in v3:
time: 76.6 us; the launch traced here: 76.1 us
  Pallas kernels  75.5 us (99%)
    pallas_call x1, Pallas kernels, per_device(): pl.pallas_call(functools.partial(legendre_kernel, N, M), out_shape=[jax.S...  58.3 us
    pallas_call x1, Pallas kernels, per_device(): pl.pallas_call(functools.partial(update_kernel, lons=lons), grid=(Q,), ou...  10.1 us
    pallas_call x1, Pallas kernels, per_device(): pl.pallas_call(synth_kernel, grid=(lons // tile,), out_shape=jax.ShapeDty...  7.09 us

profile of v3, /device:TPU:0, one launch (start us, length us, event | category | flops | bytes accessed | tf_op | source)
XLA Modules:
  0.0 76.1 jit_solution(5211481331126480459)
XLA Ops:
  0.6 10.1 %update.1 = (f32[3,4,32,2,1280]{4,3,2,1,0:T(2,128)}, bf16[8,32,1280]{2,1,0:T(8,128)(2,1)}, f32[256,128]{1,0:T(8,128)}, f32[256,128]{1,0:T(8,128)}, f32[256,128]{1,0:T(8,128)}, /*index=5*/f32[256,128]{1,0:T(8,128)}) custom-call(s32[128]{0:T(128)} %m_ref.1, f32[3]{0:T(128)} %d_ref.1, f32[3,1280]{1,0:T(4,128)} %amp_ref.1, f32[3,4,32,2,1280]{4,3,2,1,0:T(2,128)} %s_ref.1, ...), custom_call_target="tpu_custom_call" | custom-call | tf_op jit(solution)/shard_map/update/pallas_call | solution.py:382
  10.8 58.3 %legendre.1 = (bf16[4,2,2,40,128]{4,3,2,1,0:T(8,128)(2,1)}, bf16[256,5120]{1,0:T(8,128)(2,1)}) custom-call(bf16[8,32,1280]{2,1,0:T(8,128)(2,1)} %get-tuple-element.10.c_ref, bf16[8,160,1280]{2,1,0:T(8,128)(2,1)} %bitcast.3, f32[256,128]{1,0:T(8,128)} %get-tuple-element.11.u_ref, f32[256,128]{1,0:T(8,128)} %get-tuple-element.12.v_ref, ...), custom_call_target="tpu_custom_call" | custom-call | tf_op jit(solution)/shard_map/legendre/pallas_call | solution.py:406
  69.1 7.1 %synthesis.1 = bf16[4,80,5120]{2,1,0:T(8,128)(2,1)} custom-call(bf16[4,2,2,40,128]{4,3,2,1,0:T(8,128)(2,1)} %get-tuple-element.15.f_ref, bf16[256,5120]{1,0:T(8,128)(2,1)} %get-tuple-element.16.basis_ref, bf16[4,80,5120]{2,1,0:T(8,128)(2,1)} %t_ref.1), custom_call_target="tpu_custom_call" | custom-call | tf_op jit(solution)/shard_map/synthesis/pallas_call | solution.py:445

commit v4 on v3

--- a/solution.py
+++ b/solution.py
@@ -11,6 +11,7 @@
 clip_level = 0.9
 MESH = pl.DeviceIdType.MESH
 PACK = 4
+AHEAD = 2
 
 
 def tail_chunks(chunks, chips):
@@ -60,17 +61,22 @@
             src_ref=ref, dst_ref=gath.at[q, src], send_sem=ssem.at[way, q, src],
             recv_sem=rsem.at[q, src], device_id={"mem": dst}, device_id_type=MESH)
 
+    def send_own(q):
+        @pl.when(goes_up(q))
+        def _():
+            hop(0, q, me, c_ref.at[q], me + 2).start()
+
+        @pl.when(goes_down(q))
+        def _():
+            hop(1, q, me, c_ref.at[q], me - 2).start()
+
     pl.semaphore_wait(barrier, N - 1 + M - 1)
 
     @pl.loop(0, Q)
     def _(q):
-        @pl.when(goes_up(q))
-        def _():
-            hop(0, q, me, c_ref.at[q], me + 2).start()
-
-        @pl.when(goes_down(q))
-        def _():
-            hop(1, q, me, c_ref.at[q], me - 2).start()
+        @pl.when(jnp.logical_or(end, q < AHEAD))
+        def _():
+            send_own(q)
 
         @pl.when(here(q))
         def _():
@@ -111,6 +117,10 @@
 
     @pl.loop(0, steps)
     def _(s):
+        @pl.when(jnp.logical_and(jnp.logical_not(end), s + AHEAD < Q))
+        def _():
+            send_own(s + AHEAD)
+
         width = u_ref.shape[1]
         turn = lax.rem(width - s * cols, width)
         u = pltpu.roll(u_ref[...], turn, 1)
@@ -323,8 +333,18 @@
     group = lax.broadcasted_iota(jnp.int32, (8, 1), 0)
     shift = (group % 2).astype(jnp.float32) * (lons // 4)
 
-    def angle(x):
-        return (x - lons * jnp.floor(x * (1.0 / lons))) * unit
+    def cos_sin(x):
+        x = x - lons * jnp.floor(x * (1.0 / lons) + 0.5)
+        k = jnp.floor(x * (4.0 / lons) + 0.5)
+        y = (x - k * (lons // 4)) * unit
+        y2 = y * y
+        c = 1.0 + y2 * (-1.0 / 2 + y2 * (1.0 / 24 + y2 * (-1.0 / 720 + y2 * (1.0 / 40320))))
+        n = y * (1.0 + y2 * (-1.0 / 6 + y2 * (1.0 / 120 + y2 * (-1.0 / 5040 + y2 * (1.0 / 362880)))))
+        odd = jnp.abs(k) == 1.0
+        cos, sin = jnp.where(odd, n, c), jnp.where(odd, c, n)
+        cos = jnp.where(jnp.logical_or(k >= 1.0, k <= -2.0), -cos, cos)
+        sin = jnp.where(jnp.logical_or(k >= 2.0, k <= -1.0), -sin, sin)
+        return cos, sin
 
     for g in range(u_ref.shape[0] // 8):
         at = (step * (u_ref.shape[0] // 8) + g) * PACK
@@ -337,12 +357,12 @@
             far = jnp.where(group // 2 == j, lax.rem(m * 128, lons), far)
         near = near * lax.broadcasted_iota(jnp.int32, (8, 128), 1)
         far = far * lax.broadcasted_iota(jnp.int32, (8, width), 1)
-        near = angle(near.astype(jnp.float32))
-        far = angle(far.astype(jnp.float32) + shift)
-        u_ref[g * 8:(g + 1) * 8] = jnp.cos(far)
-        v_ref[g * 8:(g + 1) * 8] = -jnp.sin(far)
-        cb_ref[g * 8:(g + 1) * 8] = jnp.cos(near)
-        sb_ref[g * 8:(g + 1) * 8] = jnp.sin(near)
+        cos, sin = cos_sin(far.astype(jnp.float32) + shift)
+        u_ref[g * 8:(g + 1) * 8] = cos
+        v_ref[g * 8:(g + 1) * 8] = -sin
+        cos, sin = cos_sin(near.astype(jnp.float32))
+        cb_ref[g * 8:(g + 1) * 8] = cos
+        sb_ref[g * 8:(g + 1) * 8] = sin
 
 
 def synth_kernel(f_ref, basis_ref, t_ref, o_ref, lhs):

time: 76.6 us -> 72.9 us (0.952)
  Pallas kernels: 75.5 us -> 71.8 us
    pallas_call x1, Pallas kernels: 58.3 us -> 55 us  [per_device(): pl.pallas_call(functools.partial(legendre_kernel, N, M), out_shape=[jax.S...]
where the time goes in v4:
time: 72.9 us; the launch traced here: 72.4 us
  Pallas kernels  71.8 us (98%)
    pallas_call x1, Pallas kernels, per_device(): pl.pallas_call(functools.partial(legendre_kernel, N, M), out_shape=[jax.S...  55 us
    pallas_call x1, Pallas kernels, per_device(): pl.pallas_call(functools.partial(update_kernel, lons=lons), grid=(Q,), ou...  9.71 us
    pallas_call x1, Pallas kernels, per_device(): pl.pallas_call(synth_kernel, grid=(lons // tile,), out_shape=jax.ShapeDty...  7.09 us

profile of v4, /device:TPU:0, one launch (start us, length us, event | category | flops | bytes accessed | tf_op | source)
XLA Modules:
  0.0 72.4 jit_solution(1378722527642510536)
XLA Ops:
  0.6 9.7 %update.1 = (f32[3,4,32,2,1280]{4,3,2,1,0:T(2,128)}, bf16[8,32,1280]{2,1,0:T(8,128)(2,1)}, f32[256,128]{1,0:T(8,128)}, f32[256,128]{1,0:T(8,128)}, f32[256,128]{1,0:T(8,128)}, /*index=5*/f32[256,128]{1,0:T(8,128)}) custom-call(s32[128]{0:T(128)} %m_ref.1, f32[3]{0:T(128)} %d_ref.1, f32[3,1280]{1,0:T(4,128)} %amp_ref.1, f32[3,4,32,2,1280]{4,3,2,1,0:T(2,128)} %s_ref.1, ...), custom_call_target="tpu_custom_call" | custom-call | tf_op jit(solution)/shard_map/update/pallas_call | solution.py:402
  10.3 55.0 %legendre.1 = (bf16[4,2,2,40,128]{4,3,2,1,0:T(8,128)(2,1)}, bf16[256,5120]{1,0:T(8,128)(2,1)}) custom-call(bf16[8,32,1280]{2,1,0:T(8,128)(2,1)} %get-tuple-element.10.c_ref, bf16[8,160,1280]{2,1,0:T(8,128)(2,1)} %bitcast.3, f32[256,128]{1,0:T(8,128)} %get-tuple-element.11.u_ref, f32[256,128]{1,0:T(8,128)} %get-tuple-element.12.v_ref, ...), custom_call_target="tpu_custom_call" | custom-call | tf_op jit(solution)/shard_map/legendre/pallas_call | solution.py:426
  65.3 7.1 %synthesis.1 = bf16[4,80,5120]{2,1,0:T(8,128)(2,1)} custom-call(bf16[4,2,2,40,128]{4,3,2,1,0:T(8,128)(2,1)} %get-tuple-element.15.f_ref, bf16[256,5120]{1,0:T(8,128)(2,1)} %get-tuple-element.16.basis_ref, bf16[4,80,5120]{2,1,0:T(8,128)(2,1)} %t_ref.1), custom_call_target="tpu_custom_call" | custom-call | tf_op jit(solution)/shard_map/synthesis/pallas_call | solution.py:465
